TPU v7x, 32 devices: a whole 2x2x4 slice. The times are simulated.
32 devices in a mesh: box: 2 (over y), gx: 8 (over z, x), gy: 2 (over core).
Axes of the slice: x: 2, y: 2, z: 4, core: 2. Of those that a mesh axis runs over, the one named last changes fastest.
Arguments:
- positions: float32 [16, 4, 3, 256], P(('box', 'gx'), 'gy'), parts along dimension 0, may hold values from 0 to 18, as said below
- polarizability: float32 [16, 4, 256], P(('box', 'gx'), 'gy'), parts along dimension 0, may hold values from 0.3 to 1.5
- tile_counts: int32 [16, 4, 2], P(('box', 'gx'), 'gy'), parts along dimension 0, may hold values from 80 to 128, as said below
- molecules: int32 [16, 4, 256], P(('box', 'gx'), 'gy'), parts along dimension 0, may hold values from 0 to 170, as said below
- perm_field: float32 [16, 4, 3, 256], P(('box', 'gx'), 'gy'), parts along dimension 0, may hold values from -6 to 6
- dipoles: float32 [16, 4, 3, 256], P(('box', 'gx'), 'gy'), parts along dimension 0, may hold values from -4 to 4
- past_out: float32 [16, 4, 7, 3, 256], P(('box', 'gx'), 'gy'), parts along dimension 0, may hold values from -4 to 4
- past_res: float32 [16, 4, 7, 3, 256], P(('box', 'gx'), 'gy'), parts along dimension 0, may hold values from -15 to 15
Outputs:
- dipoles_next: float32 [16, 4, 3, 256], P(('box', 'gx'), 'gy'), parts along dimension 0
- diis_weights: float32 [16], P('box'), parts along dimension 0
There are 2 independent parts, one for each index of `box`. A program takes and returns all parts, laid end to end along the dimension named above; each array names one. Nothing has to cross between parts.
Inputs may be any that keep to these rules, and one draw needn't show every extreme that they name: x and y in [0, 9); z of an atom in z-tile t lies in [9 t, 9 t + 9); padded slots carry positions too. `tile_counts`: some z-tile is full. `molecules`: a group holds at most three atoms, all of one z-tile of one cell.
All inputs are finite; a program needn't handle non-finite values.
Results may differ from a plain program's by a relative error of at most 0.0003.
Values sent between devices are 32-bit elements; how exact they have to be, the bound alone decides.
A program may use at most 64 MiB of HBM per device.

v0:
```python
import jax
import jax.numpy as jnp
from jax import lax
from jax.sharding import PartitionSpec as P

ITERS = 2
CELL_SIDE = 9.0
CUTOFF_SQ = 81.0
SOFTENING = 0.25
THOLE_DAMP = 0.39
FAR_LIFT = 1000.0
NEIGHBOUR_X = (1.0, 0.0, 1.0, 1.0)
NEIGHBOUR_Y = (0.0, 1.0, 1.0, -1.0)


def from_behind(block, axis, distance):
    devices = range(lax.axis_size(axis))
    route = [((i - distance) % len(devices), i) for i in devices]
    return lax.ppermute(block, axis, route)


def pair_terms(
    target_coords,
    target_polar,
    target_groups,
    target_occupied,
    source_coords,
    source_polar,
    source_groups,
    source_occupied,
):
    displace = source_coords[:, None, :] - target_coords[:, :, None]
    square_dist = jnp.sum(displace * displace, axis=0) + SOFTENING
    distance = jnp.sqrt(square_dist)
    cube_dist = square_dist * distance
    damped = THOLE_DAMP * cube_dist / jnp.sqrt(target_polar[:, None] * source_polar[None, :])
    damping = jnp.exp(-damped)
    tapering = jnp.square(jnp.maximum(1.0 - square_dist / CUTOFF_SQ, 0.0))
    keeper = (target_groups[:, None] != source_groups[None, :]).astype(jnp.float32)
    weight = tapering * keeper * target_occupied[:, None] * source_occupied[None, :]
    isotropic = weight * -jnp.expm1(-damped) / cube_dist
    tensorial = 3.0 * weight * (1.0 - (1.0 + damped) * damping) / (cube_dist * square_dist)
    return (displace, isotropic, tensorial)


def field_targets(displace, isotropic, tensorial, source_dipole):
    projected = jnp.sum(displace * source_dipole[:, None, :], axis=0)
    return jnp.sum(displace * (tensorial * projected)[None], axis=2) - jnp.sum(
        isotropic[None] * source_dipole[:, None, :], axis=2
    )


def field_sources(displace, isotropic, tensorial, target_dipole):
    projected = jnp.sum(displace * target_dipole[:, :, None], axis=0)
    return jnp.sum(displace * (tensorial * projected)[None], axis=1) - jnp.sum(
        isotropic[None] * target_dipole[:, :, None], axis=1
    )


def tiled(values, filler, tile_count):
    shaped = values.reshape(values.shape[:-1] + (tile_count, values.shape[-1] // tile_count))
    widths = [(0, 0)] * (shaped.ndim - 2) + [(1, 1), (0, 0)]
    return jnp.pad(shaped, widths, constant_values=filler)


def padded_coords(coords, tile_count):
    marker = tiled(jnp.zeros_like(coords), 1.0, tile_count)
    lifted = jnp.array([0.0, 0.0, FAR_LIFT], jnp.float32).reshape(3, 1, 1)
    return tiled(coords, 0.0, tile_count) + marker * lifted


def band_sources(padded, tile_at):
    coords, polarity, groups, occupied, dipole = padded

    def flat_vector(member):
        window_part = lax.dynamic_slice_in_dim(member, tile_at, 3, 2)
        return jnp.transpose(window_part, (1, 0, 2, 3)).reshape(3, -1)

    def flat_scalar(member):
        return lax.dynamic_slice_in_dim(member, tile_at, 3, 1).reshape(-1)

    return (
        flat_vector(coords),
        flat_scalar(polarity),
        flat_scalar(groups),
        flat_scalar(occupied),
        flat_vector(dipole),
    )


def target_tile(own_cell, first_slot, tile_width):
    coords, polarity, groups, occupied = own_cell
    return (
        lax.dynamic_slice_in_dim(coords, first_slot, tile_width, 1),
        lax.dynamic_slice_in_dim(polarity, first_slot, tile_width, 0),
        lax.dynamic_slice_in_dim(groups, first_slot, tile_width, 0),
        lax.dynamic_slice_in_dim(occupied, first_slot, tile_width, 0),
    )


def four_static(packed):
    east_cells = from_behind(packed, "gx", -1)
    next_own, next_east = from_behind((packed[0], east_cells[0]), "gy", -1)
    prior_east = from_behind(east_cells[-1], "gy", 1)
    north_cells = jnp.concatenate([packed[1:], next_own[None]], axis=0)
    north_east = jnp.concatenate([east_cells[1:], next_east[None]], axis=0)
    south_east = jnp.concatenate([prior_east[None], east_cells[:-1]], axis=0)
    return jnp.stack([east_cells, north_cells, north_east, south_east], axis=1)


def four_dipole(dipole):
    east_cells = from_behind(dipole, "gx", -1)
    next_own, next_east = from_behind((dipole[0], east_cells[0]), "gy", -1)
    prior_east = from_behind(east_cells[-1], "gy", 1)
    north_cells = jnp.concatenate([dipole[1:], next_own[None]], axis=0)
    north_east = jnp.concatenate([east_cells[1:], next_east[None]], axis=0)
    south_east = jnp.concatenate([prior_east[None], east_cells[:-1]], axis=0)
    return jnp.stack([east_cells, north_cells, north_east, south_east], axis=1)


def half_statics(coords, polarity, groups, occupied, tile_count):
    cell_count = coords.shape[0]
    packed = jnp.concatenate([coords, polarity[:, None], occupied[:, None]], axis=1)
    nearby = four_static(packed)
    lift_x = jnp.array(NEIGHBOUR_X, jnp.float32) * CELL_SIDE
    lift_y = jnp.array(NEIGHBOUR_Y, jnp.float32) * CELL_SIDE
    lifted = jnp.stack([lift_x, lift_y, jnp.zeros_like(lift_x)], axis=1)
    nearby_coords = nearby[:, :, 0:3] + lifted[None, :, :, None]
    nearby_groups = jnp.full((cell_count, 4, coords.shape[-1]), -1, jnp.int32)
    own_padded = (
        padded_coords(coords[:, None], tile_count),
        tiled(polarity[:, None], 1.0, tile_count),
        tiled(groups[:, None], -1, tile_count),
        tiled(occupied[:, None], 0.0, tile_count),
    )
    nearby_padded = (
        padded_coords(nearby_coords, tile_count),
        tiled(nearby[:, :, 3], 1.0, tile_count),
        tiled(nearby_groups, -1, tile_count),
        tiled(nearby[:, :, 4], 0.0, tile_count),
    )
    return (own_padded, nearby_padded)


def half_cell(own_cell, own_band, nearby_band, dipole, tile_count):
    tile_width = dipole.shape[-1] // tile_count

    def one_tile(tile_at, carry):
        own_field, back_field = carry
        first_slot = tile_at * tile_width
        target = target_tile(own_cell, first_slot, tile_width)
        target_dipole = lax.dynamic_slice_in_dim(dipole, first_slot, tile_width, 1)
        source = band_sources(own_band, tile_at)
        displace, isotropic, tensorial = pair_terms(
            target[0], target[1], target[2], target[3], source[0], source[1], source[2], source[3]
        )
        inside = field_targets(displace, isotropic, tensorial, source[4])
        source = band_sources(nearby_band, tile_at)
        displace, isotropic, tensorial = pair_terms(
            target[0], target[1], target[2], target[3], source[0], source[1], source[2], source[3]
        )
        outside = field_targets(displace, isotropic, tensorial, source[4])
        returned = field_sources(displace, isotropic, tensorial, target_dipole)
        returned = jnp.transpose(returned.reshape(3, 4, 3, tile_width), (1, 0, 2, 3))
        own_field = lax.dynamic_update_slice_in_dim(own_field, inside + outside, first_slot, 1)
        window = lax.dynamic_slice_in_dim(back_field, tile_at, 3, 2) + returned
        back_field = lax.dynamic_update_slice_in_dim(back_field, window, tile_at, 2)
        return (own_field, back_field)

    initial = (
        jnp.zeros(dipole.shape, jnp.float32),
        jnp.zeros((4, 3, tile_count + 2, tile_width), jnp.float32),
    )
    own_field, back_field = lax.fori_loop(0, tile_count, one_tile, initial)
    return (own_field, back_field[:, :, 1:-1].reshape(4, 3, -1))


def half_field(own_cells, statics, dipole, tile_count):
    own_padded, nearby_padded = statics
    own_band = own_padded + (tiled(dipole[:, None], 0.0, tile_count),)
    nearby_band = nearby_padded + (tiled(four_dipole(dipole), 0.0, tile_count),)

    def per_cell(members):
        return half_cell(members[0], members[1], members[2], members[3], tile_count)

    own_field, back_field = lax.map(per_cell, (own_cells, own_band, nearby_band, dipole))
    north_part = back_field[:, 1]
    north_east = back_field[:, 2]
    south_east = back_field[:, 3]
    from_below, below_east = from_behind((north_part[-1], north_east[-1]), "gy", 1)
    from_above = from_behind(south_east[0], "gy", -1)
    from_south = jnp.concatenate([from_below[None], north_part[:-1]], axis=0)
    from_south_west = jnp.concatenate([below_east[None], north_east[:-1]], axis=0)
    from_north = jnp.concatenate([south_east[1:], from_above[None]], axis=0)
    eastward = back_field[:, 0] + from_south_west + from_north
    from_west = from_behind(eastward, "gx", 1)
    return own_field + from_south + from_west


def diis_weights(gram_matrix):
    lower = jnp.linalg.cholesky(gram_matrix)
    history = gram_matrix.shape[0]
    forward = []
    for row_at in range(history):
        running = jnp.ones((), gram_matrix.dtype)
        for col_at in range(row_at):
            running = running - lower[row_at, col_at] * forward[col_at]
        forward.append(running / lower[row_at, row_at])
    backward = [None] * history
    for row_at in reversed(range(history)):
        running = forward[row_at]
        for col_at in range(row_at + 1, history):
            running = running - lower[col_at, row_at] * backward[col_at]
        backward[row_at] = running / lower[row_at, row_at]
    solved = jnp.stack(backward)
    return solved / jnp.sum(solved)


def body(
    positions, polarizability, tile_counts, molecules, perm_field, dipoles, past_out, past_res
):
    counts = tile_counts[0]
    cell_count = counts.shape[0]
    tile_count = counts.shape[1]
    coords = positions[0]
    atom_slots = coords.shape[-1]
    tile_width = atom_slots // tile_count
    slot_index = lax.broadcasted_iota(jnp.int32, (cell_count, tile_count, tile_width), 2)
    occupied = (slot_index < counts[:, :, None]).astype(jnp.float32).reshape(cell_count, atom_slots)
    polarity = polarizability[0]
    groups = molecules[0]
    own_cells = (coords, polarity, groups, occupied)
    occupied_vec = occupied[:, None, :]
    scaled = occupied_vec * polarity[:, None, :]
    stored_out = jnp.moveaxis(past_out[0], 1, 0) * occupied_vec
    stored_res = jnp.moveaxis(past_res[0], 1, 0) * occupied_vec
    current = dipoles[0] * occupied_vec
    permanent = perm_field[0]
    statics = half_statics(coords, polarity, groups, occupied, tile_count)
    weights = jnp.zeros((stored_out.shape[0] + 1,), jnp.float32)
    for step_at in range(ITERS):
        induced = half_field(own_cells, statics, current, tile_count)
        jacobi = scaled * (permanent + induced)
        residual = jacobi - current
        outputs_all = jnp.concatenate([stored_out, jacobi[None]], 0)
        residual_all = jnp.concatenate([stored_res, residual[None]], 0)
        flattened = residual_all.reshape(residual_all.shape[0], -1)
        local_gram = jnp.dot(
            flattened,
            flattened.T,
            precision=lax.Precision.HIGHEST,
            preferred_element_type=jnp.float32,
        )
        gram_matrix = lax.psum(local_gram, ("gx", "gy"))
        weights = diis_weights(gram_matrix)
        current = jnp.sum(weights[:, None, None, None] * outputs_all, axis=0)
        stored_out = outputs_all[1:]
        stored_res = residual_all[1:]
    return (current[None], weights)


def solution(mesh):
    placed = (
        P(("box", "gx"), "gy", None, None),
        P(("box", "gx"), "gy", None),
        P(("box", "gx"), "gy", None),
        P(("box", "gx"), "gy", None),
        P(("box", "gx"), "gy", None, None),
        P(("box", "gx"), "gy", None, None),
        P(("box", "gx"), "gy", None, None, None),
        P(("box", "gx"), "gy", None, None, None),
    )
    return jax.shard_map(
        body,
        mesh=mesh,
        in_specs=placed,
        out_specs=(P(("box", "gx"), "gy", None, None), P("box")),
        check_vma=False,
    )
```

profile of v0, /device:TPU:0, one launch (start us, length us, event | category | flops | bytes accessed | tf_op | source)
XLA Modules:
  0.0 246.8 jit_solution(973416661079791287)
XLA Ops:
  0.7 0.8 broadcast_bitcast_fusion
  1.4 0.7 bitcast_multiply_fusion.2
  2.1 6.0 %collective-permute-start.4 = (f32[2,3,256]{2,1,0:T(4,128)S(1)}, f32[2,3,256]{2,1,0:T(4,128)S(1)}, u32[]{:S(2)}, u32[]{:S(2)}) collective-permute-start(f32[2,3,256]{2,1,0:T(4,128)S(1)} %bitcast_multiply_fusion.2), channel_id=1, source_target_pairs={{2,0},{4,2},{6,4},{8,6},{10,8},{12,10},{14,12},{0,14},{3,1},{5,3},... | collective-permute-start | bytes 18440 | tf_op jit(solution)/shard_map/ppermute | solution.py:19
  8.2 0.7 lt.120
  8.9 0.7 broadcast_in_dim_squeeze.8
  9.6 0.7 copy.384
  11.1 0.8 iota_compare_fusion.4
  11.9 0.8 compare_convert_fusion.1
  12.6 0.7 copy.283
  13.3 0.7 copy.284
  14.1 0.7 pad_bitcast_fusion
  14.8 0.7 reshape_broadcast_in_dim_squeeze.10
  15.6 0.7 reshape_broadcast_in_dim_squeeze.11
  20.0 23.1 %while.55 = (s32[]{:T(128)}, f32[2,3,256]{2,1,0:T(4,128)S(1)}, f32[2,4,3,256]{3,1,2,0:T(4,128)S(1)}, f32[2,3,256]{2,1,0:T(4,128)S(1)}, f32[2,256]{1,0:T(2,128)S(...) while((s32[]{:T(128)}, f32[2,3,256]{2,1,0:T(4,128)S(1)}, ...), condition=%wide.region_14.15_spmd, body=%wide.region_0.14_spmd.sunk | while | flops 19906180 | bytes 14344956 | solution.py:186
  20.2 11.3 %while.58 = (s32[]{:T(128)}, f32[3,256]{1,0:T(4,128)S(1)}, f32[4,3,4,128]{3,2,0,1:T(4,128)S(1)}, f32[1,3,4,128]{3,2,1,0:T(4,128)S(1)}, f32[3,256]{1,0:T(4,128)S(...) while((s32[]{:T(128)}, f32[3,256]{1,0:T(4,128)S(1)}, ...), condition=%wide.region_13.13_spmd, body=%wide.region_1.12_spmd.sunk | while | flops 19906180 | bytes 14031151 | solution.py:174
  21.9 1.0 fusion.153
  22.8 1.0 fusion.154
  23.8 1.0 fusion.155
  24.9 0.6 fusion.156
  27.5 1.0 fusion.153
  28.5 1.0 fusion.154
  29.5 1.0 fusion.155
  30.6 0.6 fusion.156
  31.7 11.3 %while.58 = (s32[]{:T(128)}, f32[3,256]{1,0:T(4,128)S(1)}, f32[4,3,4,128]{3,2,0,1:T(4,128)S(1)}, f32[1,3,4,128]{3,2,1,0:T(4,128)S(1)}, f32[3,256]{1,0:T(4,128)S(...) while((s32[]{:T(128)}, f32[3,256]{1,0:T(4,128)S(1)}, ...), condition=%wide.region_13.13_spmd, body=%wide.region_1.12_spmd.sunk | while | flops 19906180 | bytes 14031151 | solution.py:174
  33.4 1.0 fusion.153
  34.4 1.0 fusion.154
  35.4 1.0 fusion.155
  36.5 0.6 fusion.156
  39.0 1.0 fusion.153
  40.0 1.0 fusion.154
  41.0 1.0 fusion.155
  42.1 0.6 fusion.156
  44.7 1.5 collective-permute-start.11
  46.2 4.8 %collective-permute-done.11 = f32[2,3,256]{2,1,0:T(4,128)S(1)} collective-permute-done((f32[2,3,256]{2,1,0:T(4,128)S(1)}, f32[2,3,256]{2,1,0:T(4,128)S(1)}, u32[]{:S(2)}, u32[]{:S(2)}) %collective-permute-start.11) | collective-permute-done | bytes 6176 | tf_op jit(solution)/shard_map/ppermute | solution.py:19
  51.3 29.5 %psum.14 = f32[8,8]{0,1:T(8,128)S(1)} all-reduce(f32[8,8]{0,1:T(8,128)S(1)} %convolution_bitcast_fusion.1), channel_id=1, replica_groups=mesh['box'=2,'gx'=8,'gy'=2] {'gx','gy'}, use_global_device_ids=true, to_apply=%region_15.16 | all-reduce | flops 64 | bytes 512 | tf_op jit(solution)/shard_map/psum | solution.py:254
  80.9 0.7 cholesky.44
  81.6 0.6 compare_reduce_fusion.1
  82.3 0.6 fusion.88
  82.9 0.7 fusion.107
  83.6 0.7 fusion.106
  130.7 3.5 %collective-permute-done.12 = f32[2,3,256]{2,1,0:T(4,128)S(1)} collective-permute-done((f32[2,3,256]{2,1,0:T(4,128)S(1)}, f32[2,3,256]{2,1,0:T(4,128)S(1)}, u32[]{:S(2)}, u32[]{:S(2)}) %collective-permute-start.12) | collective-permute-done | bytes 6176 | tf_op jit(solution)/shard_map/ppermute | solution.py:19
  135.7 23.1 %while.57 = (s32[]{:T(128)}, f32[2,3,256]{2,1,0:T(4,128)S(1)}, f32[2,4,3,256]{3,1,2,0:T(4,128)S(1)}, f32[2,3,256]{2,1,0:T(4,128)S(1)}, f32[2,256]{1,0:T(2,128)S(...) while((s32[]{:T(128)}, f32[2,3,256]{2,1,0:T(4,128)S(1)}, ...), condition=%wide.region_33.35_spmd, body=%wide.region_19.34_spmd.sunk | while | flops 19906180 | bytes 14344960 | solution.py:186
  135.9 11.3 %while.59 = (s32[]{:T(128)}, f32[3,256]{1,0:T(4,128)S(1)}, f32[4,3,4,128]{3,2,0,1:T(4,128)S(1)}, f32[1,3,4,128]{3,2,1,0:T(4,128)S(1)}, f32[3,256]{1,0:T(4,128)S(...) while((s32[]{:T(128)}, f32[3,256]{1,0:T(4,128)S(1)}, ...), condition=%wide.region_32.33_spmd, body=%wide.region_20.32_spmd.sunk | while | flops 19906180 | bytes 14031151 | solution.py:174
  137.6 1.0 fusion.143
  138.6 1.0 fusion.144
  139.6 1.0 fusion.145
  143.2 1.0 fusion.143
  144.2 1.0 fusion.144
  145.2 1.0 fusion.145
  146.3 0.6 fusion.146
  147.5 11.3 %while.59 = (s32[]{:T(128)}, f32[3,256]{1,0:T(4,128)S(1)}, f32[4,3,4,128]{3,2,0,1:T(4,128)S(1)}, f32[1,3,4,128]{3,2,1,0:T(4,128)S(1)}, f32[3,256]{1,0:T(4,128)S(...) while((s32[]{:T(128)}, f32[3,256]{1,0:T(4,128)S(1)}, ...), condition=%wide.region_32.33_spmd, body=%wide.region_20.32_spmd.sunk | while | flops 19906180 | bytes 14031151 | solution.py:174
  149.2 1.0 fusion.143
  150.2 1.0 fusion.144
  151.2 1.0 fusion.145
  154.8 1.0 fusion.143
  155.8 1.0 fusion.144
  156.8 1.0 fusion.145
  160.7 6.1 %collective-permute-done.19 = f32[2,3,256]{2,1,0:T(4,128)S(1)} collective-permute-done((f32[2,3,256]{2,1,0:T(4,128)S(1)}, f32[2,3,256]{2,1,0:T(4,128)S(1)}, u32[]{:S(2)}, u32[]{:S(2)}) %collective-permute-start.19) | collective-permute-done | bytes 6176 | tf_op jit(solution)/shard_map/ppermute | solution.py:19
  167.1 29.5 %psum.15 = f32[8,8]{0,1:T(8,128)S(1)} all-reduce(f32[8,8]{0,1:T(8,128)S(1)} %convolution_bitcast_fusion), channel_id=1, replica_groups=mesh['box'=2,'gx'=8,'gy'=2] {'gx','gy'}, use_global_device_ids=true, to_apply=%region_34.36 | all-reduce | flops 64 | bytes 512 | tf_op jit(solution)/shard_map/psum | solution.py:254
  196.7 0.7 cholesky.55
  197.4 0.6 compare_reduce_fusion
  198.1 0.6 select_select_fusion
  198.7 0.7 fusion.105
  199.4 0.7 fusion.104
  (432 shorter events, 29.0 us)
Async XLA Ops:
  0.6 19.1 %copy-start.6 = (f32[3]{0:T(128)S(1)}, f32[3]{0:T(128)}, u32[]{:S(2)}) copy-start(f32[3]{0:T(128)} %constant.290.clone) | copy-start | bytes 40
  0.6 18.9 %copy-start.7 = (f32[4,3]{1,0:T(4,128)S(1)}, f32[4,3]{1,0:T(4,128)}, u32[]{:S(2)}) copy-start(f32[4,3]{1,0:T(4,128)} %constant.329) | copy-start | bytes 148
  0.7 19.3 %copy-start = (f32[1,2,256]{2,1,0:T(2,128)S(1)}, f32[1,2,256]{2,1,0:T(2,128)}, u32[]{:S(2)}) copy-start(f32[1,2,256]{2,1,0:T(2,128)} %param.22) | copy-start | bytes 6148
  0.7 19.3 %copy-start.1 = (s32[1,2,256]{2,1,0:T(2,128)S(1)}, s32[1,2,256]{2,1,0:T(2,128)}, u32[]{:S(2)}) copy-start(s32[1,2,256]{2,1,0:T(2,128)} %param.24) | copy-start | bytes 6148
  2.1 14.2 %collective-permute-start.4 = (f32[2,3,256]{2,1,0:T(4,128)S(1)}, f32[2,3,256]{2,1,0:T(4,128)S(1)}, u32[]{:S(2)}, u32[]{:S(2)}) collective-permute-start(f32[2,3,256]{2,1,0:T(4,128)S(1)} %bitcast_multiply_fusion.2), channel_id=1, source_target_pairs={{2,0},{4,2},{6,4},{8,6},{10,8},{12,10},{14,12},{0,14},{3,1},{5,3},... | collective-permute-start | bytes 18440 | tf_op jit(solution)/shard_map/ppermute | solution.py:19
  8.2 8.2 %collective-permute-start.5 = (f32[3,256]{1,0:T(4,128)S(1)}, f32[3,256]{1,0:T(4,128)S(1)}, u32[]{:S(2)}, u32[]{:S(2)}) collective-permute-start(f32[3,256]{1,0:T(4,128)S(1)} %get-tuple-element.1237), channel_id=1, source_target_pairs={{1,0},{0,1},{3,2},{2,3},{5,4},{4,5},{7,6},{6,7},{9,8},{8,9},{11,10... | collective-permute-start | bytes 9224 | tf_op jit(solution)/shard_map/ppermute | solution.py:19
  10.3 7.6 %collective-permute-start = (f32[2,5,256]{2,1,0:T(8,128)S(1)}, f32[2,5,256]{2,1,0:T(8,128)S(1)}, u32[]{:S(2)}, u32[]{:S(2)}) collective-permute-start(f32[2,5,256]{2,1,0:T(8,128)S(1)} %pad_maximum_fusion.4), channel_id=1, source_target_pairs={{2,0},{4,2},{6,4},{8,6},{10,8},{12,10},{14,12},{0,14},{3,1},{5,3},... | collective-permute-start | bytes 30728 | tf_op jit(solution)/shard_map/ppermute | solution.py:19
  10.9 6.1 %collective-permute-start.1 = (f32[5,256]{1,0:T(8,128)S(1)}, f32[5,256]{1,0:T(8,128)S(1)}, u32[]{:S(2)}, u32[]{:S(2)}) collective-permute-start(f32[5,256]{1,0:T(8,128)S(1)} %get-tuple-element.1225), channel_id=1, source_target_pairs={{1,0},{0,1},{3,2},{2,3},{5,4},{4,5},{7,6},{6,7},{9,8},{8,9},{11,10... | collective-permute-start | bytes 15368 | tf_op jit(solution)/shard_map/ppermute | solution.py:19
  16.4 1.2 collective-permute-start.7
  16.7 1.2 collective-permute-start.6
  17.9 1.2 collective-permute-start.3
  18.3 1.2 collective-permute-start.2
  19.9 23.8 %copy-start.3 = (f32[1,2,7,3,256]{4,1,3,2,0:T(2,128)S(1)}, f32[1,2,7,3,256]{4,1,3,2,0:T(2,128)}, u32[]{:S(2)}) copy-start(f32[1,2,7,3,256]{4,1,3,2,0:T(2,128)} %param.28) | copy-start | bytes 129028
  19.9 23.8 %copy-start.4 = (f32[1,2,7,3,256]{4,1,3,2,0:T(2,128)S(1)}, f32[1,2,7,3,256]{4,1,3,2,0:T(2,128)}, u32[]{:S(2)}) copy-start(f32[1,2,7,3,256]{4,1,3,2,0:T(2,128)} %param.27) | copy-start | bytes 129028
  19.9 31.1 %copy-start.2 = (f32[1,2,3,256]{3,1,2,0:T(2,128)S(1)}, f32[1,2,3,256]{3,1,2,0:T(2,128)}, u32[]{:S(2)}) copy-start(f32[1,2,3,256]{3,1,2,0:T(2,128)} %param.26) | copy-start | bytes 18436
  20.0 31.1 %copy-start.5 = (f32[1,2,3,256]{3,1,2,0:T(2,128)S(1)}, f32[1,2,3,256]{3,1,2,0:T(2,128)}, u32[]{:S(2)}) copy-start(f32[1,2,3,256]{3,1,2,0:T(2,128)} %param.25) | copy-start | bytes 18436
  43.1 1.2 collective-permute-start.10
  43.5 1.2 collective-permute-start.9
  43.7 2.5 collective-permute-start.8
  44.7 6.4 %collective-permute-start.11 = (f32[2,3,256]{2,1,0:T(4,128)S(1)}, f32[2,3,256]{2,1,0:T(4,128)S(1)}, u32[]{:S(2)}, u32[]{:S(2)}) collective-permute-start(f32[2,3,256]{2,1,0:T(4,128)S(1)} %fusion.77), channel_id=1, source_target_pairs={{14,0},{0,2},{2,4},{4,6},{6,8},{8,10},{10,12},{12,14},{15,1},{1,3}... | collective-permute-start | bytes 18440 | tf_op jit(solution)/shard_map/ppermute | solution.py:19
  130.4 3.9 %collective-permute-start.12 = (f32[2,3,256]{2,1,0:T(4,128)S(1)}, f32[2,3,256]{2,1,0:T(4,128)S(1)}, u32[]{:S(2)}, u32[]{:S(2)}) collective-permute-start(f32[2,3,256]{2,1,0:T(4,128)S(1)} %fusion.59), channel_id=1, source_target_pairs={{2,0},{4,2},{6,4},{8,6},{10,8},{12,10},{14,12},{0,14},{3,1},{5,3},... | collective-permute-start | bytes 18440 | tf_op jit(solution)/shard_map/ppermute | solution.py:19
  130.7 4.2 %collective-permute-start.13 = (f32[3,256]{1,0:T(4,128)S(1)}, f32[3,256]{1,0:T(4,128)S(1)}, u32[]{:S(2)}, u32[]{:S(2)}) collective-permute-start(f32[3,256]{1,0:T(4,128)S(1)} %get-tuple-element.1231), channel_id=1, source_target_pairs={{1,0},{0,1},{3,2},{2,3},{5,4},{4,5},{7,6},{6,7},{9,8},{8,9},{11,10... | collective-permute-start | bytes 9224 | tf_op jit(solution)/shard_map/ppermute | solution.py:19
  134.3 1.2 collective-permute-start.15
  134.3 1.3 collective-permute-start.14
  158.9 1.2 collective-permute-start.18
  159.3 1.2 collective-permute-start.17
  159.5 1.2 collective-permute-start.16
  160.5 6.4 %collective-permute-start.19 = (f32[2,3,256]{2,1,0:T(4,128)S(1)}, f32[2,3,256]{2,1,0:T(4,128)S(1)}, u32[]{:S(2)}, u32[]{:S(2)}) collective-permute-start(f32[2,3,256]{2,1,0:T(4,128)S(1)} %fusion.75), channel_id=1, source_target_pairs={{14,0},{0,2},{2,4},{4,6},{6,8},{8,10},{10,12},{12,14},{15,1},{1,3}... | collective-permute-start | bytes 18440 | tf_op jit(solution)/shard_map/ppermute | solution.py:19
  246.1 0.7 copy-start.8
where the time goes:
time: 249 us; the launch traced here: 247 us
  between operations  92.8 us (37%)
  blocking collectives  59 us (24%)
  other arithmetic  47 us (19%)
  waiting for transfers between devices  18.3 us (7%)
  local copies, waits for them, and re-layouts  15.3 us (6%)
  starting transfers between devices  12.4 us (5%)
    psum x2, blocking collectives, body(): gram_matrix = lax.psum(local_gram, ('gx', 'gy'))  59 us
    ppermute x20, waiting for transfers between devices, from_behind(): return lax.ppermute(block, axis, route)  18.3 us
    ppermute x20, starting transfers between devices, from_behind(): return lax.ppermute(block, axis, route)  12.4 us
    div x16, other arithmetic, pair_terms(): isotropic = weight * -jnp.expm1(-damped) / cube_dist  10.8 us
    reduce_sum x8, other arithmetic, field_sources(): projected = jnp.sum(displace * target_dipole[:, :, None], axis=0)  8.01 us
    mul x8, other arithmetic, field_targets(): tensorial * projected  7.77 us
    reduce_sum x8, other arithmetic, field_sources(): jnp.sum(displace * (tensorial * projected)[None], axis=1)  5.08 us
  transfers between devices with their start and end apart: 20, of which 14 were waited for; matrix products, arithmetic and copies ran while one was open for 3% of the time, Pallas kernels for 0%

commit v1 on v0

--- a/solution.py
+++ b/solution.py
@@ -251,7 +251,7 @@
             precision=lax.Precision.HIGHEST,
             preferred_element_type=jnp.float32,
         )
-        gram_matrix = lax.psum(local_gram, ("gx", "gy"))
+        gram_matrix = jnp.sum(lax.all_gather(local_gram, ("gx", "gy")), axis=0)
         weights = diis_weights(gram_matrix)
         current = jnp.sum(weights[:, None, None, None] * outputs_all, axis=0)
         stored_out = outputs_all[1:]

time: 249 us -> 226 us (0.908)
  blocking collectives: 59 us -> 36.6 us
  waiting for transfers between devices: 18.3 us -> 13.4 us
  starting transfers between devices: 12.4 us -> 17.2 us
    psum x2 -> x0, blocking collectives: 59 us -> none  [body(): gram_matrix = lax.psum(local_gram, ('gx', 'gy'))]
    all_gather x0 -> x2, blocking collectives: none -> 36.6 us  [body(): gram_matrix = jnp.sum(lax.all_gather(local_gram, ('gx', 'gy')), axis=0)]
    ppermute x20, starting transfers between devices: 12.4 us -> 17.2 us  [from_behind(): return lax.ppermute(block, axis, route)]
    ppermute x20, waiting for transfers between devices: 18.3 us -> 13.4 us  [from_behind(): return lax.ppermute(block, axis, route)]
  transfers between devices with their start and end apart: 20 -> 20, of which waited for: 14 -> 13; matrix products, arithmetic and copies ran while one was open for 3% -> 3% of each run, Pallas kernels for 0% -> 0%
where the time goes in v1:
time: 226 us; the launch traced here: 224 us
  between operations  92.8 us (41%)
  other arithmetic  47.1 us (21%)
  blocking collectives  36.6 us (16%)
  starting transfers between devices  17.2 us (8%)
  local copies, waits for them, and re-layouts  15.3 us (7%)
  waiting for transfers between devices  13.4 us (6%)
    all_gather x2, blocking collectives, body(): gram_matrix = jnp.sum(lax.all_gather(local_gram, ('gx', 'gy')), axis=0)  36.6 us
    ppermute x20, starting transfers between devices, from_behind(): return lax.ppermute(block, axis, route)  17.2 us
    ppermute x20, waiting for transfers between devices, from_behind(): return lax.ppermute(block, axis, route)  13.4 us
    div x16, other arithmetic, pair_terms(): isotropic = weight * -jnp.expm1(-damped) / cube_dist  10.8 us
    reduce_sum x8, other arithmetic, field_sources(): projected = jnp.sum(displace * target_dipole[:, :, None], axis=0)  8.01 us
    mul x8, other arithmetic, field_targets(): tensorial * projected  7.77 us
    reduce_sum x8, other arithmetic, field_sources(): jnp.sum(displace * (tensorial * projected)[None], axis=1)  5.08 us
  transfers between devices with their start and end apart: 20, of which 13 were waited for; matrix products, arithmetic and copies ran while one was open for 3% of the time, Pallas kernels for 0%

profile of v1, /device:TPU:0, one launch (start us, length us, event | category | flops | bytes accessed | tf_op | source)
XLA Modules:
  0.0 224.4 jit_solution(10350353775158289384)
XLA Ops:
  0.7 0.8 broadcast_bitcast_fusion
  1.4 0.7 bitcast_multiply_fusion.2
  2.1 6.0 %collective-permute-start.4 = (f32[2,3,256]{2,1,0:T(4,128)S(1)}, f32[2,3,256]{2,1,0:T(4,128)S(1)}, u32[]{:S(2)}, u32[]{:S(2)}) collective-permute-start(f32[2,3,256]{2,1,0:T(4,128)S(1)} %bitcast_multiply_fusion.2), channel_id=1, source_target_pairs={{2,0},{4,2},{6,4},{8,6},{10,8},{12,10},{14,12},{0,14},{3,1},{5,3},... | collective-permute-start | bytes 18440 | tf_op jit(solution)/shard_map/ppermute | solution.py:19
  8.2 0.7 lt.120
  8.9 0.7 broadcast_in_dim_squeeze.8
  9.6 0.7 copy.368
  11.1 0.8 iota_compare_fusion.4
  11.9 0.8 compare_convert_fusion.1
  12.6 0.7 copy.271
  13.3 0.7 copy.272
  14.1 0.7 pad_bitcast_fusion
  14.8 0.7 reshape_broadcast_in_dim_squeeze.10
  15.6 0.7 reshape_broadcast_in_dim_squeeze.11
  20.0 23.1 %while.55 = (s32[]{:T(128)}, f32[2,3,256]{2,1,0:T(4,128)S(1)}, f32[2,4,3,256]{3,1,2,0:T(4,128)S(1)}, f32[2,3,256]{2,1,0:T(4,128)S(1)}, f32[2,256]{1,0:T(2,128)S(...) while((s32[]{:T(128)}, f32[2,3,256]{2,1,0:T(4,128)S(1)}, ...), condition=%wide.region_14.15_spmd, body=%wide.region_0.14_spmd.sunk | while | flops 19906180 | bytes 14344956 | solution.py:186
  20.2 11.3 %while.58 = (s32[]{:T(128)}, f32[3,256]{1,0:T(4,128)S(1)}, f32[4,3,4,128]{3,2,0,1:T(4,128)S(1)}, f32[1,3,4,128]{3,2,1,0:T(4,128)S(1)}, f32[3,256]{1,0:T(4,128)S(...) while((s32[]{:T(128)}, f32[3,256]{1,0:T(4,128)S(1)}, ...), condition=%wide.region_13.13_spmd, body=%wide.region_1.12_spmd.sunk | while | flops 19906180 | bytes 14031151 | solution.py:174
  21.9 1.0 fusion.153
  22.8 1.0 fusion.154
  23.8 1.0 fusion.155
  24.9 0.6 fusion.156
  27.5 1.0 fusion.153
  28.5 1.0 fusion.154
  29.5 1.0 fusion.155
  30.6 0.6 fusion.156
  31.7 11.3 %while.58 = (s32[]{:T(128)}, f32[3,256]{1,0:T(4,128)S(1)}, f32[4,3,4,128]{3,2,0,1:T(4,128)S(1)}, f32[1,3,4,128]{3,2,1,0:T(4,128)S(1)}, f32[3,256]{1,0:T(4,128)S(...) while((s32[]{:T(128)}, f32[3,256]{1,0:T(4,128)S(1)}, ...), condition=%wide.region_13.13_spmd, body=%wide.region_1.12_spmd.sunk | while | flops 19906180 | bytes 14031151 | solution.py:174
  33.4 1.0 fusion.153
  34.4 1.0 fusion.154
  35.4 1.0 fusion.155
  36.5 0.6 fusion.156
  39.0 1.0 fusion.153
  40.0 1.0 fusion.154
  41.0 1.0 fusion.155
  44.7 1.5 collective-permute-start.11
  46.2 4.8 %collective-permute-done.11 = f32[2,3,256]{2,1,0:T(4,128)S(1)} collective-permute-done((f32[2,3,256]{2,1,0:T(4,128)S(1)}, f32[2,3,256]{2,1,0:T(4,128)S(1)}, u32[]{:S(2)}, u32[]{:S(2)}) %collective-permute-start.11) | collective-permute-done | bytes 6176 | tf_op jit(solution)/shard_map/ppermute | solution.py:19
  51.3 17.3 %all-gather = f32[128,8]{1,0:T(8,128)S(1)} all-gather(f32[8,8]{1,0:T(8,128)S(1)} %convolution_bitcast_fusion.1), channel_id=2, replica_groups=mesh['box'=2,'gx'=8,'gy'=2] {'gx','gy'}, dimensions={0}, use_global_device_ids=true | all-gather | bytes 4352 | tf_op jit(solution)/shard_map/all_gather | solution.py:254
  68.7 0.7 cholesky.44
  69.4 0.6 compare_reduce_fusion.1
  70.1 0.6 fusion.88
  70.7 0.7 fusion.107
  71.4 0.7 fusion.106
  118.2 2.2 collective-permute-start.12
  120.5 1.6 collective-permute-done.12
  123.5 23.1 %while.57 = (s32[]{:T(128)}, f32[2,3,256]{2,1,0:T(4,128)S(1)}, f32[2,4,3,256]{3,1,2,0:T(4,128)S(1)}, f32[2,3,256]{2,1,0:T(4,128)S(1)}, f32[2,256]{1,0:T(2,128)S(...) while((s32[]{:T(128)}, f32[2,3,256]{2,1,0:T(4,128)S(1)}, ...), condition=%wide.region_33.35_spmd, body=%wide.region_19.34_spmd.sunk | while | flops 19906180 | bytes 14344960 | solution.py:186
  123.8 11.3 %while.59 = (s32[]{:T(128)}, f32[3,256]{1,0:T(4,128)S(1)}, f32[4,3,4,128]{3,2,0,1:T(4,128)S(1)}, f32[1,3,4,128]{3,2,1,0:T(4,128)S(1)}, f32[3,256]{1,0:T(4,128)S(...) while((s32[]{:T(128)}, f32[3,256]{1,0:T(4,128)S(1)}, ...), condition=%wide.region_32.33_spmd, body=%wide.region_20.32_spmd.sunk | while | flops 19906180 | bytes 14031151 | solution.py:174
  125.4 1.0 fusion.143
  126.4 1.0 fusion.144
  127.4 1.0 fusion.145
  131.1 1.0 fusion.143
  132.1 1.0 fusion.144
  133.1 1.0 fusion.145
  135.3 11.3 %while.59 = (s32[]{:T(128)}, f32[3,256]{1,0:T(4,128)S(1)}, f32[4,3,4,128]{3,2,0,1:T(4,128)S(1)}, f32[1,3,4,128]{3,2,1,0:T(4,128)S(1)}, f32[3,256]{1,0:T(4,128)S(...) while((s32[]{:T(128)}, f32[3,256]{1,0:T(4,128)S(1)}, ...), condition=%wide.region_32.33_spmd, body=%wide.region_20.32_spmd.sunk | while | flops 19906180 | bytes 14031151 | solution.py:174
  137.0 1.0 fusion.143
  138.0 1.0 fusion.144
  139.0 1.0 fusion.145
  142.6 1.0 fusion.143
  143.6 1.0 fusion.144
  144.6 1.0 fusion.145
  148.3 2.9 %collective-permute-start.19 = (f32[2,3,256]{2,1,0:T(4,128)S(1)}, f32[2,3,256]{2,1,0:T(4,128)S(1)}, u32[]{:S(2)}, u32[]{:S(2)}) collective-permute-start(f32[2,3,256]{2,1,0:T(4,128)S(1)} %fusion.75), channel_id=1, source_target_pairs={{14,0},{0,2},{2,4},{4,6},{6,8},{8,10},{10,12},{12,14},{15,1},{1,3}... | collective-permute-start | bytes 18440 | tf_op jit(solution)/shard_map/ppermute | solution.py:19
  151.3 3.4 %collective-permute-done.19 = f32[2,3,256]{2,1,0:T(4,128)S(1)} collective-permute-done((f32[2,3,256]{2,1,0:T(4,128)S(1)}, f32[2,3,256]{2,1,0:T(4,128)S(1)}, u32[]{:S(2)}, u32[]{:S(2)}) %collective-permute-start.19) | collective-permute-done | bytes 6176 | tf_op jit(solution)/shard_map/ppermute | solution.py:19
  154.9 19.3 %all-gather.1 = f32[128,8]{1,0:T(8,128)S(1)} all-gather(f32[8,8]{1,0:T(8,128)S(1)} %convolution_bitcast_fusion), channel_id=3, replica_groups=mesh['box'=2,'gx'=8,'gy'=2] {'gx','gy'}, dimensions={0}, use_global_device_ids=true | all-gather | bytes 4352 | tf_op jit(solution)/shard_map/all_gather | solution.py:254
  174.3 0.7 cholesky.55
  175.0 0.6 compare_reduce_fusion
  175.7 0.6 select_select_fusion
  176.3 0.7 fusion.105
  177.0 0.7 fusion.104
  (434 shorter events, 29.8 us)
Async XLA Ops:
  0.6 19.1 %copy-start.6 = (f32[3]{0:T(128)S(1)}, f32[3]{0:T(128)}, u32[]{:S(2)}) copy-start(f32[3]{0:T(128)} %constant.290.clone) | copy-start | bytes 40
  0.6 18.9 %copy-start.7 = (f32[4,3]{1,0:T(4,128)S(1)}, f32[4,3]{1,0:T(4,128)}, u32[]{:S(2)}) copy-start(f32[4,3]{1,0:T(4,128)} %constant.329) | copy-start | bytes 148
  0.7 19.3 %copy-start = (f32[1,2,256]{2,1,0:T(2,128)S(1)}, f32[1,2,256]{2,1,0:T(2,128)}, u32[]{:S(2)}) copy-start(f32[1,2,256]{2,1,0:T(2,128)} %param.22) | copy-start | bytes 6148
  0.7 19.3 %copy-start.1 = (s32[1,2,256]{2,1,0:T(2,128)S(1)}, s32[1,2,256]{2,1,0:T(2,128)}, u32[]{:S(2)}) copy-start(s32[1,2,256]{2,1,0:T(2,128)} %param.24) | copy-start | bytes 6148
  2.1 14.2 %collective-permute-start.4 = (f32[2,3,256]{2,1,0:T(4,128)S(1)}, f32[2,3,256]{2,1,0:T(4,128)S(1)}, u32[]{:S(2)}, u32[]{:S(2)}) collective-permute-start(f32[2,3,256]{2,1,0:T(4,128)S(1)} %bitcast_multiply_fusion.2), channel_id=1, source_target_pairs={{2,0},{4,2},{6,4},{8,6},{10,8},{12,10},{14,12},{0,14},{3,1},{5,3},... | collective-permute-start | bytes 18440 | tf_op jit(solution)/shard_map/ppermute | solution.py:19
  8.2 8.2 %collective-permute-start.5 = (f32[3,256]{1,0:T(4,128)S(1)}, f32[3,256]{1,0:T(4,128)S(1)}, u32[]{:S(2)}, u32[]{:S(2)}) collective-permute-start(f32[3,256]{1,0:T(4,128)S(1)} %get-tuple-element.1237), channel_id=1, source_target_pairs={{1,0},{0,1},{3,2},{2,3},{5,4},{4,5},{7,6},{6,7},{9,8},{8,9},{11,10... | collective-permute-start | bytes 9224 | tf_op jit(solution)/shard_map/ppermute | solution.py:19
  10.3 7.6 %collective-permute-start = (f32[2,5,256]{2,1,0:T(8,128)S(1)}, f32[2,5,256]{2,1,0:T(8,128)S(1)}, u32[]{:S(2)}, u32[]{:S(2)}) collective-permute-start(f32[2,5,256]{2,1,0:T(8,128)S(1)} %pad_maximum_fusion.4), channel_id=1, source_target_pairs={{2,0},{4,2},{6,4},{8,6},{10,8},{12,10},{14,12},{0,14},{3,1},{5,3},... | collective-permute-start | bytes 30728 | tf_op jit(solution)/shard_map/ppermute | solution.py:19
  10.9 6.1 %collective-permute-start.1 = (f32[5,256]{1,0:T(8,128)S(1)}, f32[5,256]{1,0:T(8,128)S(1)}, u32[]{:S(2)}, u32[]{:S(2)}) collective-permute-start(f32[5,256]{1,0:T(8,128)S(1)} %get-tuple-element.1225), channel_id=1, source_target_pairs={{1,0},{0,1},{3,2},{2,3},{5,4},{4,5},{7,6},{6,7},{9,8},{8,9},{11,10... | collective-permute-start | bytes 15368 | tf_op jit(solution)/shard_map/ppermute | solution.py:19
  16.4 1.2 collective-permute-start.7
  16.7 1.2 collective-permute-start.6
  17.9 1.2 collective-permute-start.3
  18.3 1.2 collective-permute-start.2
  19.9 23.8 %copy-start.3 = (f32[1,2,7,3,256]{4,1,3,2,0:T(2,128)S(1)}, f32[1,2,7,3,256]{4,1,3,2,0:T(2,128)}, u32[]{:S(2)}) copy-start(f32[1,2,7,3,256]{4,1,3,2,0:T(2,128)} %param.28) | copy-start | bytes 129028
  19.9 23.8 %copy-start.4 = (f32[1,2,7,3,256]{4,1,3,2,0:T(2,128)S(1)}, f32[1,2,7,3,256]{4,1,3,2,0:T(2,128)}, u32[]{:S(2)}) copy-start(f32[1,2,7,3,256]{4,1,3,2,0:T(2,128)} %param.27) | copy-start | bytes 129028
  19.9 31.1 %copy-start.2 = (f32[1,2,3,256]{3,1,2,0:T(2,128)S(1)}, f32[1,2,3,256]{3,1,2,0:T(2,128)}, u32[]{:S(2)}) copy-start(f32[1,2,3,256]{3,1,2,0:T(2,128)} %param.26) | copy-start | bytes 18436
  20.0 31.1 %copy-start.5 = (f32[1,2,3,256]{3,1,2,0:T(2,128)S(1)}, f32[1,2,3,256]{3,1,2,0:T(2,128)}, u32[]{:S(2)}) copy-start(f32[1,2,3,256]{3,1,2,0:T(2,128)} %param.25) | copy-start | bytes 18436
  43.1 1.2 collective-permute-start.10
  43.5 1.2 collective-permute-start.9
  43.7 2.5 %collective-permute-start.8 = (f32[3,256]{1,0:T(4,128)S(1)}, f32[3,256]{1,0:T(4,128)S(1)}, u32[]{:S(2)}, u32[]{:S(2)}) collective-permute-start(f32[3,256]{1,0:T(4,128)S(1)} %get-tuple-element.1218), channel_id=1, source_target_pairs={{1,0},{0,1},{3,2},{2,3},{5,4},{4,5},{7,6},{6,7},{9,8},{8,9},{11,10... | collective-permute-start | bytes 9224 | tf_op jit(solution)/shard_map/ppermute | solution.py:19
  44.7 6.4 %collective-permute-start.11 = (f32[2,3,256]{2,1,0:T(4,128)S(1)}, f32[2,3,256]{2,1,0:T(4,128)S(1)}, u32[]{:S(2)}, u32[]{:S(2)}) collective-permute-start(f32[2,3,256]{2,1,0:T(4,128)S(1)} %fusion.77), channel_id=1, source_target_pairs={{14,0},{0,2},{2,4},{4,6},{6,8},{8,10},{10,12},{12,14},{15,1},{1,3}... | collective-permute-start | bytes 18440 | tf_op jit(solution)/shard_map/ppermute | solution.py:19
  118.2 3.9 %collective-permute-start.12 = (f32[2,3,256]{2,1,0:T(4,128)S(1)}, f32[2,3,256]{2,1,0:T(4,128)S(1)}, u32[]{:S(2)}, u32[]{:S(2)}) collective-permute-start(f32[2,3,256]{2,1,0:T(4,128)S(1)} %fusion.59), channel_id=1, source_target_pairs={{2,0},{4,2},{6,4},{8,6},{10,8},{12,10},{14,12},{0,14},{3,1},{5,3},... | collective-permute-start | bytes 18440 | tf_op jit(solution)/shard_map/ppermute | solution.py:19
  120.5 2.2 collective-permute-start.13
  122.1 1.2 collective-permute-start.15
  122.1 1.3 collective-permute-start.14
  146.7 1.2 collective-permute-start.18
  147.1 1.2 collective-permute-start.17
  147.3 3.9 %collective-permute-start.16 = (f32[3,256]{1,0:T(4,128)S(1)}, f32[3,256]{1,0:T(4,128)S(1)}, u32[]{:S(2)}, u32[]{:S(2)}) collective-permute-start(f32[3,256]{1,0:T(4,128)S(1)} %get-tuple-element.1213), channel_id=1, source_target_pairs={{1,0},{0,1},{3,2},{2,3},{5,4},{4,5},{7,6},{6,7},{9,8},{8,9},{11,10... | collective-permute-start | bytes 9224 | tf_op jit(solution)/shard_map/ppermute | solution.py:19
  148.3 6.4 %collective-permute-start.19 = (f32[2,3,256]{2,1,0:T(4,128)S(1)}, f32[2,3,256]{2,1,0:T(4,128)S(1)}, u32[]{:S(2)}, u32[]{:S(2)}) collective-permute-start(f32[2,3,256]{2,1,0:T(4,128)S(1)} %fusion.75), channel_id=1, source_target_pairs={{14,0},{0,2},{2,4},{4,6},{6,8},{8,10},{10,12},{12,14},{15,1},{1,3}... | collective-permute-start | bytes 18440 | tf_op jit(solution)/shard_map/ppermute | solution.py:19
  223.7 0.7 copy-start.8
